TPU v7x, 32 devices: a whole 2x2x4 slice. The times are simulated.
32 devices in a mesh: rep: 4 (over y, x), grp: 8 (over z, core).
Axes of the slice: x: 2, y: 2, z: 4, core: 2. Of those that a mesh axis runs over, the one named last changes fastest.
Arguments:
- block_in: bfloat16 [2, 4, 1024, 1024], P(None, 'rep', 'grp'), may hold values from -6 to 6
- cotangent: bfloat16 [2, 4, 1024, 1024], P(None, 'rep', 'grp'), may hold values from -6 to 6
- w_qkv: bfloat16 [2, 1024, 3072], P(None, 'grp'), may hold values from -0.1875 to 0.1875
- w_out: bfloat16 [2, 1024, 1024], P(None, 'grp'), may hold values from -0.1875 to 0.1875
- w_up: bfloat16 [2, 1024, 4096], P(None, 'grp'), may hold values from -0.1875 to 0.1875
- w_down: bfloat16 [2, 4096, 1024], P(None, 'grp'), may hold values from -0.09375 to 0.09375
- norm_gains: bfloat16 [2, 1024, 4], P(None, 'grp'), may hold values from 0.25 to 1.75
Outputs:
- block_out: bfloat16 [2, 4, 1024, 1024], P(None, 'rep', 'grp')
- block_in_grad: float32 [2, 4, 1024, 1024], P(None, 'rep', 'grp')
- w_qkv_grad: float32 [2, 1024, 3072], P(None, 'grp')
- w_out_grad: float32 [2, 1024, 1024], P(None, 'grp')
- w_up_grad: float32 [2, 1024, 4096], P(None, 'grp')
- w_down_grad: float32 [2, 4096, 1024], P(None, 'grp')
- norm_gains_grad: float32 [2, 1024, 4], P(None, 'grp')
All inputs are finite; a program needn't handle non-finite values.
Results may differ from a plain program's by a relative error of at most 0.023.
Values may be sent and summed in bfloat16 or wider, within the bound.
A program may use at most 384 MiB of HBM per device.

v0:
```python
import functools
import types

import jax
import jax.numpy as jnp
from jax import lax
from jax.experimental import pallas as pl
from jax.experimental.pallas import tpu as pltpu
from jax.sharding import PartitionSpec as P

HEADS = 16
HDIM = 64
EPS = 1e-06
NEGATIVE = -1e30
BF = jnp.bfloat16
REP, GRP = "rep", "grp"
F32 = jnp.float32


def dot(left, right):
    return jnp.dot(left, right, preferred_element_type=F32)


def dot_tn(left, right):
    return lax.dot_general(left, right, (((0,), (0,)), ((), ())), preferred_element_type=F32)


def dot_nt(left, right):
    return lax.dot_general(left, right, (((1,), (1,)), ((), ())), preferred_element_type=F32)


def norm(values, gain):
    return values * lax.rsqrt(jnp.mean(values * values, axis=-1, keepdims=True) + EPS) * gain


def head_mask(width, head):
    lanes = lax.broadcasted_iota(jnp.int32, (1, width), 1)
    return (lanes // HDIM) == head


def causal_scores(query, keys, below, start):
    scores = dot_nt(query, keys)
    last = jnp.where(below, scores[:, start:], NEGATIVE)
    return jnp.concatenate([scores[:, :start], last], axis=1) if start else last


def each_head(heads, one_head, tick):
    half = heads // 2 if tick else heads
    for first in range(0, heads, half):
        loop(half, lambda index: one_head(index + first))
        if tick and first == 0:
            tick()


def attend(ns, stream, block=256):
    length, width = ns.mixed_v.shape
    qkv_ref, lse_ref, sum_ref = ns.qkv_in_v, ns.lse_v, ns.terms_own.at[stream]
    row = lax.broadcasted_iota(jnp.int32, (block, block), 0)
    col = lax.broadcasted_iota(jnp.int32, (block, block), 1)
    below = col <= row
    zero = jnp.zeros((), BF)
    lane = lax.broadcasted_iota(jnp.int32, (1, 128), 1)
    base, high = stream * length // 2, (stream + 1) * length // 2
    sum_ref[...] = jnp.zeros_like(sum_ref)
    lse_ref[base:high, :] = jnp.zeros((length // 2, 128), F32)

    def one_head(head):
        mask = head_mask(width, head)
        for start in range(base, high, block):
            stop = start + block
            query = qkv_ref[start:stop, :width] * jnp.asarray(HDIM**-0.5, BF)
            query = jnp.where(mask, query, zero)
            scores = causal_scores(query, qkv_ref[:stop, width : 2 * width], below, start)
            top = jnp.max(scores, axis=1, keepdims=True)
            terms = jnp.exp(scores - top)
            sums = jnp.sum(terms, axis=1, keepdims=True)
            mixed = dot(terms.astype(BF), qkv_ref[:stop, 2 * width :]) * (1.0 / sums)
            sum_ref[:, start - base : stop - base] += jnp.where(mask, mixed, 0.0)
            stats = lse_ref[start:stop, :]
            lse_ref[start:stop, :] = jnp.where(lane == head, top + jnp.log(sums), stats)

    each_head(width // HDIM, one_head, None)
    for start in range(base, high, block):
        ns.mixed_v[start : start + block, :] = sum_ref[:, start - base : start - base + width].astype(BF)


def attend_back(ns, stream, tick, block=256):
    length, width = ns.mixed_grad_v.shape
    qkv_ref, grad_ref, sum_ref = ns.qkv_in_v, ns.mixed_grad_v, ns.terms_own.at[stream]
    row = lax.broadcasted_iota(jnp.int32, (block, block), 0)
    col = lax.broadcasted_iota(jnp.int32, (block, block), 1)
    below = col <= row
    zero = jnp.zeros((), BF)
    scale = HDIM**-0.5
    lane = lax.broadcasted_iota(jnp.int32, (1, 128), 1)
    base, high = stream * length // 2, (stream + 1) * length // 2
    sum_ref[...] = jnp.zeros_like(sum_ref)

    def one_head(head):
        mask = head_mask(width, head)
        for start in range(base, high, block):
            stop = start + block
            query = qkv_ref[start:stop, :width] * jnp.asarray(scale, BF)
            query = jnp.where(mask, query, zero)
            grad = jnp.where(mask, grad_ref[start:stop, :], zero)
            keys, vals = qkv_ref[:stop, width : 2 * width], qkv_ref[:stop, 2 * width :]
            scores = causal_scores(query, keys, below, start)
            lse = jnp.where(lane == head, ns.lse_v[start:stop, :], 0.0)
            probs = jnp.exp(scores - jnp.sum(lse, axis=1, keepdims=True))
            prob_grad = dot_nt(grad, vals)
            delta = jnp.sum(probs * prob_grad, axis=1, keepdims=True)
            score_grad = (probs * (prob_grad - delta)).astype(BF)
            query_grad = jnp.where(mask, dot(score_grad, keys), 0.0)
            sum_ref[:, start - base : stop - base] += query_grad
            ns.dk_v[:stop, :] += dot_tn(score_grad, query)
            ns.dv_v[:stop, :] += dot_tn(probs.astype(BF), grad)

    each_head(width // HDIM, one_head, tick)
    for start in range(base, high, block):
        value = sum_ref[:, start - base : start - base + width] * scale
        ns.qkv_grad_v[start : start + block, :width] = value.astype(BF)
    ns.qkv_grad_v[base:high, width : 2 * width] = ns.dk_v[base:high, :].astype(BF)
    ns.qkv_grad_v[base:high, 2 * width :] = ns.dv_v[base:high, :].astype(BF)


MESH_ID = pl.DeviceIdType.MESH
HELD, ONE, TWO, SUM, LINE, FULL = "_v", "one", "two", "sum", "line", "full"
PASSED = ("give", "take", "send", "got")
ATTN, DOWN, UP, QKV = "attn", "down", "up", "qkv"
D0, U0, Q0, O0 = "d0", "u0", "q0", "o0"
D1, U1, Q1, O1 = "d1", "u1", "q1", "o1"
TOK = 128


class Place:
    def __init__(self):
        rep, grp = lax.axis_index(REP), lax.axis_index(GRP)
        self.rep, self.grp = rep, grp
        self.x, self.y = lax.rem(rep, 2), lax.div(rep, 2)
        self.t, self.upper = lax.rem(grp, 4), lax.div(grp, 4)
        self.c, self.side = lax.rem(grp, 2), lax.div(self.t, 2)
        base = self.upper * 4
        self.core = (rep, base + self.side * 2 + 1 - self.c)
        self.near = (rep, base + (1 - self.side) * 2 + self.c)
        self.far = (rep, (1 - self.upper) * 4 + self.t)
        self.along_x = (self.y * 2 + 1 - self.x, grp)
        self.along_y = ((1 - self.y) * 2 + self.x, grp)
        self.near_t = (1 - self.side) * 2 + self.c

    def line(self, offset):
        c = 1 - self.c if offset & 1 else self.c
        side = 1 - self.side if offset & 2 else self.side
        upper = 1 - self.upper if offset & 4 else self.upper
        return (self.rep, upper * 4 + side * 2 + c), upper, side * 2 + c


class Copies:
    def __init__(self, send, recv, here):
        self.sems, self.here = (send, recv), here
        self.sent, self.local_count, self.stores = [], 0, []

    def remote(self, source, target, device):
        at = len(self.sent)
        assert at < self.sems[0].shape[0]
        copy = pltpu.make_async_remote_copy(
            src_ref=source,
            dst_ref=target,
            send_sem=self.sems[0].at[at],
            recv_sem=self.sems[1].at[at],
            device_id=device,
            device_id_type=MESH_ID,
        )
        copy.start()
        self.sent.append(copy)
        return copy

    def local(self, source, target):
        assert self.local_count < self.here.shape[0]
        copy = pltpu.make_async_copy(source, target, self.here.at[self.local_count])
        self.local_count += 1
        copy.start()
        return copy

    def store(self, source, target):
        self.stores.append(self.local(source, target))

    def finish(self):
        for copy in self.sent:
            copy.wait_send()
        for copy in self.stores:
            copy.wait()


def meet(devices):
    barrier = pltpu.get_barrier_semaphore()
    for device in devices:
        pl.semaphore_signal(barrier, inc=1, device_id=device, device_id_type=MESH_ID)
    pl.semaphore_wait(barrier, len(devices))


class Plan:
    def __init__(self, *entries):
        self.entries = list(entries)

    def tick(self):
        if self.entries:
            for action in self.entries.pop(0):
                action()

    def drain(self):
        while self.entries:
            self.tick()


def stages(task):
    return lambda: next(task, None)


def spread(copies, place, part, last=True):
    x, y, every = place.x, place.y, slice(None)
    one = copies.remote(part(0, y, x), part(0, y, x), place.along_x)
    two = copies.remote(part(1, y, x), part(1, y, x), place.along_y)
    yield
    one.wait_recv()
    three = copies.remote(part(0, y, every), part(0, y, every), place.along_y)
    two.wait_recv()
    four = copies.remote(part(1, every, x), part(1, every, x), place.along_x)
    yield
    three.wait_recv()
    four.wait_recv()
    if last:
        yield


def deal(copies, place, source, target):
    moved = []
    own = copies.local(source.at[place.t], target)
    for offset in range(1, 8):
        if offset == 4:
            yield
        device, upper, t = place.line(offset)
        moved.append(copies.remote(source.at[t], target, device))
    yield
    own.wait()
    for copy in moved:
        copy.wait_recv()
    yield


def add_low(one, two):
    return (one.astype(F32) + two.astype(F32)).astype(BF)


def reduce_rep(copies, place, grad, ns, name):
    x, y = place.x, place.y
    count = grad.shape[1]

    def step_one():
        one = getattr(ns, name + ONE)
        first = copies.remote(grad.at[0, :, :, 1 - x], one.at[0], place.along_x)
        second = copies.remote(grad.at[1, :, 1 - y], one.at[1], place.along_y)
        yield
        first.wait_recv()
        second.wait_recv()
        for i in range(count):
            for j in range(2):
                grad[0, i, j, x] = add_low(grad[0, i, j, x], one[0, i, j])
                grad[1, i, y, j] = add_low(grad[1, i, y, j], one[1, i, j])
        yield

    def step_two():
        two, total = getattr(ns, name + TWO), getattr(ns, name + SUM)
        first = copies.remote(grad.at[0, :, 1 - y, x], two.at[0], place.along_y)
        second = copies.remote(grad.at[1, :, y, 1 - x], two.at[1], place.along_x)
        own = [copies.local(grad.at[half, :, y, x], total.at[half]) for half in range(2)]
        yield
        first.wait_recv()
        second.wait_recv()
        for half in range(2):
            own[half].wait()
            for i in range(count):
                total[half, i] = add_low(total[half, i], two[half, i])
        yield

    return step_one(), step_two()


def line_columns(copies, place, ns, name):
    total, line, full = (getattr(ns, name + part) for part in (SUM, LINE, FULL))
    moved = []
    for offset in range(1, 8):
        device, upper, t = place.line(offset)
        here = line.at[place.upper, place.t]
        moved.append(copies.remote(total.at[upper, t], here, device))
    line[place.upper, place.t] = total[place.upper, place.t]
    yield
    for copy in moved:
        copy.wait_recv()
    for t in range(4):
        full[place.y, place.x, t] = add_low(line[0, t], line[1, t])
    yield


def line_rows(copies, place, ns, name):
    total, line, full = (getattr(ns, name + part) for part in (SUM, LINE, FULL))
    moved = copies.remote(total.at[1 - place.upper, 0], line, place.far)
    yield
    moved.wait_recv()
    rows = line.shape[0] // 2
    for half in range(2):
        at = pl.ds(half * rows, rows)
        full[place.y, place.x, half] = add_low(total[place.upper, 0, at, :], line[at, :])
    yield


def whole_columns(copies, place, ns, name, target, groups):
    full = getattr(ns, name + FULL)
    yield from spread(copies, place, lambda half, a, b: full.at[a, b, pl.ds(2 * half, 2)], False)
    unit = full.shape[4] // groups
    for t in range(4):
        for k in range(groups):
            source = full.at[:, :, t, :, k * unit : (k + 1) * unit]
            start = (k * 4 + t) * unit
            copies.store(source, target.at[:, :, :, start : start + unit])
    yield


def whole_rows(copies, place, ns, name, target):
    full = getattr(ns, name + FULL)
    yield from spread(copies, place, lambda half, a, b: full.at[a, b, half], False)
    copies.store(full, target)
    yield


def reduce_scratch(name, count, rows, width, steps=3):
    total = {}
    if steps & 1:
        total[name + ONE] = pltpu.VMEM((2, count, 2, rows, width), BF)
    if steps & 2:
        total[name + TWO] = pltpu.VMEM((2, count, rows, width), BF)
        total[name + SUM] = pltpu.VMEM((2, count, rows, width), BF)
    return total


def finish_scratch(name, count, rows, width):
    if count == 1:
        line, full = (rows, width), (2, 2, 2, rows // 2, width)
    else:
        line, full = (2, count, rows, width), (2, 2, count, rows, width)
    return {name + LINE: pltpu.VMEM(line, BF), name + FULL: pltpu.VMEM(full, BF)}


def by_device(shape, count):
    rows, width = shape
    return struct((2, count, 2, 2, rows // (8 * count), width), BF)


def loop(count, step):
    def run(index, carry):
        step(index)
        return carry

    lax.fori_loop(0, count, run, 0)


def tile_of(index, size):
    return pl.ds(pl.multiple_of(index * size, size), size)


def matrix(value):
    return value.reshape(-1, value.shape[-1])


def times(left, right_ref, tile, sink):
    every = (slice(None),) * (len(right_ref.shape) - 1)

    def step(index):
        at = tile_of(index, tile)
        sink(at, dot(left(), matrix(right_ref[(*every, at)])))

    loop(right_ref.shape[-1] // tile, step)


def times_rows(left, right_ref, tile, sink):
    flat = len(right_ref.shape) == 2

    def step(index):
        if flat:
            at = tile_of(index, tile)
            sink(at, dot_nt(left(), right_ref[at, :]))
        else:
            block = matrix(right_ref[index])
            sink(tile_of(index, block.shape[0]), dot_nt(left(), block))

    loop(right_ref.shape[0] // (tile if flat else 1), step)


def gram(left_ref, right_ref, out_ref):
    count, tile = out_ref.shape[1], 256
    total = left_ref.shape[1]
    if total == tile:
        value = dot_tn(left_ref[...], right_ref[...]).astype(BF)
        out_ref[...] = value.reshape(out_ref.shape)
        return

    def step(index):
        value = dot_tn(left_ref[:, tile_of(index, tile)], right_ref[...]).astype(BF)
        half, part = lax.div(index, 2), lax.rem(index, 2)
        if count == 1:
            out_ref[half, 0, part] = value.reshape(out_ref.shape[3:])
        else:
            out_ref[half, pl.ds(part * 2, 2)] = value.reshape(2, *out_ref.shape[2:])

    loop(total // tile, step)


class Gather:
    def __init__(self, copies, place, buf, order=(0, 1)):
        self.copies, self.place, self.buf, self.order = copies, place, buf, order
        self.flight = {}

    def rows(self, stream, where):
        start = (self.order[stream] * 4 + where) * TOK
        return pl.ds(pl.multiple_of(start, TOK), TOK)

    def pair(self, stream, side):
        start = (self.order[stream] * 4 + side * 2) * TOK
        return pl.ds(pl.multiple_of(start, TOK), 2 * TOK)

    def start(self, stream, block):
        at = self.rows(stream, self.place.t)
        self.buf[at, :] = block
        mine = self.buf.at[at, :]
        across = self.copies.remote(mine, mine, self.place.near)
        beside = self.copies.remote(mine, mine, self.place.core)
        self.flight[stream] = [across, beside]

    def wait_chip(self, stream):
        self.flight[stream][1].wait_recv()

    def forward(self, stream):
        self.flight[stream][0].wait_recv()
        got = self.buf.at[self.rows(stream, self.place.near_t), :]
        self.flight[stream].append(self.copies.remote(got, got, self.place.core))

    def wait_rest(self, stream):
        self.flight[stream][2].wait_recv()


class Scatter:
    def __init__(self, copies, place, ns, name):
        self.copies, self.place = copies, place
        self.away, self.own = ns.terms_away, ns.terms_own
        self.give, self.take, self.send, self.got = (
            getattr(ns, name + part) for part in PASSED
        )
        self.flight = {}

    def push(self, stream, product):
        place, copies = self.place, self.copies
        mine = pl.ds(pl.multiple_of(place.c * TOK, TOK), TOK)
        other = pl.ds(pl.multiple_of((1 - place.c) * TOK, TOK), TOK)

        def to_away(at, value):
            self.away[:, at] = value

        def to_own(at, value):
            self.own[stream, :, at] = value

        product(1 - place.side, to_away)
        self.give[stream, 0] = self.away[other, :].astype(BF)
        first = copies.remote(self.give.at[stream, 0], self.take.at[stream, 0], place.core)
        product(place.side, to_own)
        first.wait_recv()
        self.send[stream] = (self.away[mine, :] + self.take[stream, 0].astype(F32)).astype(BF)
        across = copies.remote(self.send.at[stream], self.got.at[stream], place.near)
        self.give[stream, 1] = self.own[stream, other, :].astype(BF)
        second = copies.remote(self.give.at[stream, 1], self.take.at[stream, 1], place.core)
        self.flight[stream] = (second, across)

    def result(self, stream):
        second, across = self.flight[stream]
        mine = pl.ds(pl.multiple_of(self.place.c * TOK, TOK), TOK)
        second.wait_recv()
        total = self.own[stream, mine, :] + self.take[stream, 1].astype(F32)
        across.wait_recv()
        return total + self.got[stream].astype(F32)


def scatter_scratch(name, width):
    give, take, send, got = (name + part for part in PASSED)
    return {
        "terms_away": pltpu.VMEM((2 * TOK, width), F32),
        "terms_own": pltpu.VMEM((2, 2 * TOK, width), F32),
        give: pltpu.VMEM((2, 2, TOK, width), BF),
        take: pltpu.VMEM((2, 2, TOK, width), BF),
        send: pltpu.VMEM((2, TOK, width), BF),
        got: pltpu.VMEM((2, TOK, width), BF),
    }


def gelu_both(x):
    cubic = x * x * 0.044715
    bent = jnp.tanh(0.7978845608028654 * (x + cubic * x))
    half = 0.5 * (1.0 + bent)
    slope = half + 0.5 * x * (1.0 - bent * bent) * (0.7978845608028654 * (1.0 + 3.0 * cubic))
    return x * half, slope


def norm_back_in(values, gain, grad):
    rstd = lax.rsqrt(jnp.mean(values * values, axis=-1, keepdims=True) + EPS)
    hat = values * rstd
    scaled = grad * gain
    back = rstd * (scaled - hat * jnp.mean(scaled * hat, axis=-1, keepdims=True))
    return back, jnp.sum(grad * hat, axis=0, keepdims=True)


def next_qkv(ns, place, blocks, tick, wait_weights, order=(0, 1), late=None):
    gather = Gather(ns.copies, place, ns.normed_v, order)
    for stream in range(2):
        if late and stream == 1:
            late()
        gather.start(stream, blocks[stream]())
        tick()
    if late:
        for stream in range(2):
            gather.forward(stream)
            tick()
    wait_weights()
    for stream in range(2):

        def project(side):
            at = gather.pair(stream, side)

            def sink(cols, value):
                ns.qkv_v[at, cols] = value.astype(BF)

            times(lambda: ns.normed_v[at, :], ns.wq_v, 384, sink)

        gather.wait_chip(stream)
        project(place.side)
        if not late:
            gather.forward(stream)
        gather.wait_rest(stream)
        project(1 - place.side)
        tick()
        here = pl.ds(pl.multiple_of(order[stream] * 4 * TOK, 4 * TOK), 4 * TOK)
        ns.copies.store(ns.normed_v.at[here, :], ns.normed.at[here, :])
        ns.copies.store(ns.qkv_v.at[here, :], ns.qkv.at[here, :])


def fwd_mid(ns, place, gain, tick, wait_out, wait_up, wait_down):
    copies = ns.copies
    attn = Scatter(copies, place, ns, ATTN)
    down = Scatter(copies, place, ns, DOWN)
    gather = Gather(copies, place, ns.mlp_v)
    wo, wu, wd = ns.wo_v, ns.wu_v, ns.wd_v
    for stream in range(2):

        def product(side, sink):
            at = gather.pair(stream, side)
            times(lambda: ns.mixed_v[at, :], wo, 512, sink)

        attend(ns, stream)
        tick()
        if stream == 0:
            wait_out()
        attn.push(stream, product)
        tick()
    ns.load.hidden.wait()
    for stream in range(2):
        value = attn.result(stream)
        ns.attn_out_v[stream] = value
        resid = ns.hidden_v[stream].astype(F32) + norm(value, gain(1))
        ns.resid_v[stream] = resid
        gather.start(stream, norm(resid, gain(2)).astype(BF))
        tick()
    wait_up()
    for stream in range(2):

        def expand(side):
            at = gather.pair(stream, side)

            def sink(cols, value):
                active, slope = gelu_both(value)
                ns.active_v[at, cols] = active.astype(BF)
                ns.slope_v[at, cols] = slope.astype(BF)

            times(lambda: ns.mlp_v[at, :], wu, 256, sink)

        gather.wait_chip(stream)
        expand(place.side)
        gather.forward(stream)
        gather.wait_rest(stream)
        expand(1 - place.side)
        if stream == 0:
            wait_down()

        def product(side, sink):
            at = gather.pair(stream, side)
            times(lambda: ns.active_v[at, :], wd, 512, sink)

        down.push(stream, product)
        tick()
    return down


def bwd_mid(ns, place, layer, grads, tick, on_down, on_up, order=(0, 1)):
    copies, gain, base = ns.copies, rows_of(ns, layer), layer * 4
    up = Scatter(copies, place, ns, UP)
    first = Gather(copies, place, ns.down_grad_v)
    second = Gather(copies, place, ns.attn_grad_v)
    wo, wu, wd = ns.wo_v, ns.wu_v, ns.wd_v
    for stream in order:
        grad = grads[stream]()
        ns.grad_v[stream] = grad
        back, four = norm_back_in(ns.down_out_v[stream], gain(3), grad)
        ns.dg_v[base + 3 : base + 4, :] += four
        first.start(stream, back.astype(BF))
        tick()
    for stream in order:

        def shrink(side):
            at = first.pair(stream, side)

            def sink(cols, value):
                slope = ns.slope_v[at, cols].astype(F32)
                ns.up_grad_v[at, cols] = (value * slope).astype(BF)

            times_rows(lambda: ns.down_grad_v[at, :], wd, 512, sink)

        first.wait_chip(stream)
        shrink(place.side)
        first.forward(stream)
        first.wait_rest(stream)
        shrink(1 - place.side)

        def product(side, sink):
            at = first.pair(stream, side)
            times_rows(lambda: ns.up_grad_v[at, :], wu, 512, sink)

        up.push(stream, product)
        tick()
    for stream in order:
        back, three = norm_back_in(ns.resid_v[stream], gain(2), up.result(stream))
        grad = ns.grad_v[stream] + back
        ns.grad_v[stream] = grad
        ns.dg_v[base + 2 : base + 3, :] += three
        back, two = norm_back_in(ns.attn_out_v[stream], gain(1), grad)
        ns.dg_v[base + 1 : base + 2, :] += two
        second.start(stream, back.astype(BF))
        tick()
        if stream == order[0]:
            gram(ns.active_v, ns.down_grad_v, ns.gd_v)
            on_down()
        else:
            gram(ns.mlp_v, ns.up_grad_v, ns.gu_v)
            on_up()
            tick()
    copies.store(ns.grad_v, ns.resid_grad)
    for stream in order:

        def project(side):
            at = second.pair(stream, side)
            ns.mixed_grad_v[at, :] = dot_nt(ns.attn_grad_v[at, :], matrix(wo[...])).astype(BF)

        second.wait_chip(stream)
        project(place.side)
        second.forward(stream)
        second.wait_rest(stream)
        project(1 - place.side)
        tick()
        here = pl.ds(stream * 4 * TOK, 4 * TOK)
        copies.store(ns.mixed_grad_v.at[here, :], ns.mixed_grad.at[here, :])
    gram(ns.mixed_v, ns.attn_grad_v, ns.go_v)


def bwd_head(ns, place, layer, tick, on_qkv, weight_first):
    copies, gain = ns.copies, rows_of(ns, layer)
    qkv = Scatter(copies, place, ns, QKV)
    walk = Gather(copies, place, None)

    def weight():
        ns.load.normed.wait()
        gram(ns.normed_v, ns.qkv_grad_v, ns.gq_v)
        on_qkv()
        tick()

    ns.dk_v[...] = jnp.zeros_like(ns.dk_v)
    ns.dv_v[...] = jnp.zeros_like(ns.dv_v)
    for stream in (1, 0):

        def product(side, sink):
            at = walk.pair(stream, side)
            times_rows(lambda: ns.qkv_grad_v[at, :], ns.wq_v, 512, sink)

        attend_back(ns, stream, tick if stream == 1 else None)
        tick()
        if stream == 1:
            ns.load.wq.wait()
        elif weight_first:
            weight()
        qkv.push(stream, product)
        tick()
    if not weight_first:
        weight()
    ns.load.hidden.wait()
    ns.load.grad.wait()

    def result(stream):
        back, one = norm_back_in(ns.hidden_v[stream].astype(F32), gain(0), qkv.result(stream))
        ns.dg_v[layer * 4 : layer * 4 + 1, :] += one
        return ns.grad_v[stream] + back

    return [functools.partial(result, stream) for stream in range(2)]


def kernel_of(body, inputs, outputs, scratch, slot, remotes, locals_, vmem, flops):
    names = [*inputs, *outputs, *scratch]

    def kernel(*refs):
        ns = types.SimpleNamespace(**dict(zip(names, refs)))
        ns.copies = Copies(*refs[len(names) :])
        ns.load = types.SimpleNamespace()
        for name in inputs:
            if name + HELD in scratch:
                copy = ns.copies.local(getattr(ns, name), getattr(ns, name + HELD))
                setattr(ns.load, name, copy)
        body(ns)
        ns.copies.finish()

    moved = sum(v.size * v.dtype.itemsize for v in [*inputs.values(), *outputs.values()])
    return kernel, dict(
        name=body.__name__,
        out_shape=list(outputs.values()),
        in_specs=[pl.BlockSpec(memory_space=pl.ANY)] * len(inputs),
        out_specs=[pl.BlockSpec(memory_space=pl.ANY)] * len(outputs),
        scratch_shapes=[
            *scratch.values(),
            pltpu.SemaphoreType.DMA((remotes,)),
            pltpu.SemaphoreType.DMA((remotes,)),
            pltpu.SemaphoreType.DMA((locals_,)),
        ],
        compiler_params=pltpu.CompilerParams(
            collective_id=slot, has_side_effects=True, vmem_limit_bytes=vmem << 20
        ),
        cost_estimate=pl.CostEstimate(flops=flops, bytes_accessed=moved, transcendentals=0),
    )


def named(outputs, results):
    return types.SimpleNamespace(**dict(zip(outputs, results)))


def held(*groups):
    merged = {name: value for group in groups for name, value in group.items()}
    return {name + HELD: pltpu.VMEM(value.shape, value.dtype) for name, value in merged.items()}


def struct(shape, dtype):
    return jax.ShapeDtypeStruct(shape, dtype)


def rows_of(ns, layer):
    return lambda index, level=layer: ns.gains_v[level * 4 + index : level * 4 + index + 1, :]


def quarter_of(ns, place, weight, layer, target):
    rows = weight.shape[1] // 4
    at = pl.ds(pl.multiple_of(place.rep * rows, rows), rows)
    return ns.copies.local(weight.at[layer, at, :], target)


def arrange(quarter, dealt, groups):
    unit = quarter.shape[1] // (groups * 4)
    for t in range(4):
        for k in range(groups):
            start = (k * 4 + t) * unit
            dealt[t, :, k * unit : (k + 1) * unit] = quarter[:, start : start + unit]


def by_rows(ref, place):
    return lambda half, a, b: ref.at[1 - place.upper, a, b, half]


def by_columns(ref):
    return lambda half, a, b: ref.at[half, :, a, b]


def start_kernel(block, gain_part, w_qkv, w_up, w_out):
    width, part = block.shape[2], w_qkv.shape[2] // 4
    units = w_up.shape[2] // 4
    length, rows = 8 * TOK, width // 32
    inputs = dict(block=block, gain_part=gain_part, w_qkv=w_qkv, w_up=w_up, w_out=w_out)
    gains = struct((gain_part.shape[0], width), F32)
    hidden = struct(block.shape, BF)
    normed = struct((length, width), BF)
    qkv = struct((length, part), BF)
    wq = struct((2, 4, 2, 2, rows, part), BF)
    outputs = dict(
        hidden=hidden,
        gains=gains,
        normed=normed,
        qkv=qkv,
        wq=wq,
        part_u=struct((2, 4, rows, units), BF),
        half_o=struct(w_out.shape[1:], BF),
    )
    kept = dict(
        half_o=struct(w_out.shape[1:], BF),
        hidden=hidden,
        gains=gains,
        normed=normed,
        qkv=qkv,
        wq=wq,
        quarter_q=struct((rows, 4 * part), BF),
        quarter_u=struct((rows, 4 * units), BF),
        deal_q=struct((4, rows, part), BF),
        deal_u=struct((4, rows, units), BF),
    )
    scratch = held(kept)

    def start(ns):
        place, copies = Place(), ns.copies
        upper, y, x = place.upper, place.y, place.x
        columns = pl.ds(pl.multiple_of(place.grp * TOK, TOK), TOK)
        line = [place.line(offset)[0] for offset in range(1, 8)]
        quarter_q = quarter_of(ns, place, ns.w_qkv, 0, ns.quarter_q_v)
        quarter_u = quarter_of(ns, place, ns.w_up, 0, ns.quarter_u_v)
        kept = copies.local(ns.block.at[upper], ns.hidden_v.at[upper])
        gain_own = copies.local(ns.gain_part, ns.gains_v.at[:, columns])
        quarter_q.wait()
        arrange(ns.quarter_q_v, ns.deal_q_v, 6)
        meet([*line, place.along_x, place.along_y])
        gain_rest = [copies.remote(ns.gain_part, ns.gains_v.at[:, columns], at) for at in line]
        wq_dealt = deal(copies, place, ns.deal_q_v, ns.wq_v.at[upper, place.t, y, x])
        next(wq_dealt)
        next(wq_dealt)
        brought = copies.remote(ns.block.at[1 - upper], ns.hidden_v.at[upper], place.far)
        out_in = copies.remote(ns.w_out.at[0, y, x], ns.half_o_v.at[y, x], place.far)
        wq_spread = spread(copies, place, by_columns(ns.wq_v))
        out_spread = spread(copies, place, lambda half, a, b: ns.half_o_v.at[a, b, half])
        up_dealt = deal(copies, place, ns.deal_u_v, ns.part_u.at[upper, place.t])
        quarter_u.wait()
        arrange(ns.quarter_u_v, ns.deal_u_v, 2)
        next(up_dealt)
        kept.wait()
        gain_own.wait()
        for copy in gain_rest:
            copy.wait_recv()

        def late():
            next(wq_spread)
            brought.wait_recv()
            copies.store(ns.hidden_v, ns.hidden)

        def out_arrived():
            out_in.wait_recv()
            next(out_spread)

        def wait_weights():
            next(wq_spread)
            copies.store(ns.wq_v, ns.wq)

        copies.store(ns.gains_v, ns.gains)
        order = (upper, 1 - upper)
        blocks = [
            functools.partial(
                lambda s: norm(ns.hidden_v[s].astype(F32), ns.gains_v[0:1, :]).astype(BF), stream
            )
            for stream in order
        ]
        plan = Plan(
            [stages(wq_dealt), stages(wq_spread)],
            [stages(up_dealt)],
            [out_arrived],
            [stages(out_spread)],
        )
        next_qkv(ns, place, blocks, plan.tick, wait_weights, order, late)
        next(out_spread)
        copies.store(ns.half_o_v, ns.half_o)
        next(up_dealt)

    flops = 2 * length * width * part
    kernel, options = kernel_of(start, inputs, outputs, scratch, 0, 48, 64, 60, flops)
    results = pl.pallas_call(kernel, **options)(*inputs.values())
    return named(outputs, results)


def forward_kernel(begun, w_qkv, w_up, w_down, w_out):
    hidden, gains = begun.hidden, begun.gains
    length, part = begun.qkv.shape
    width, mixed_width = hidden.shape[2], part // 3
    units, rows = w_up.shape[2] // 4, width // 32
    inputs = dict(
        qkv_in=begun.qkv, hidden=hidden, gains=gains, w_qkv=w_qkv, w_up=w_up, w_down=w_down,
        w_out=w_out, part_u=begun.part_u, half_o=begun.half_o,
    )
    blocks = struct((2, TOK, width), F32)
    wide = struct((length, width), BF)
    next_u, next_o = struct((2, 4, rows, units), BF), struct((2, *w_out.shape[1:]), BF)
    outputs = dict(
        mixed=struct((length, mixed_width), BF),
        lse=struct((length, 128), F32),
        attn_out=blocks,
        resid=blocks,
        mlp=wide,
        active=struct((length, units), BF),
        slope=struct((length, units), BF),
        down_out=blocks,
        hidden_out=blocks,
        normed=wide,
        qkv=struct((length, part), BF),
        wu=struct((2, 4, 2, 2, rows, units), BF),
        wd=struct((2, *w_down.shape[1:]), BF),
        wo=next_o,
        wq=struct((2, 4, 2, 2, rows, part), BF),
    )
    kept = dict(
        qkv_in=begun.qkv,
        hidden=hidden,
        gains=gains,
        quarter_q=struct((rows, 4 * part), BF),
        quarter_u=struct((rows, 4 * units), BF),
        deal_q=struct((4, rows, part), BF),
        deal_u=struct((4, rows, units), BF),
    )
    scratch = held(outputs, kept)
    outputs = dict(outputs, next_u=next_u, next_o=next_o)
    scratch |= scatter_scratch(ATTN, width) | scatter_scratch(DOWN, width)

    def forward(ns):
        place, copies = Place(), ns.copies
        upper, t, y, x = place.upper, place.t, place.y, place.x
        half_o = copies.local(ns.half_o, ns.wo_v.at[1 - upper])
        part_u = copies.local(ns.part_u, ns.wu_v.at[:, :, y, x])
        quarter_q = quarter_of(ns, place, ns.w_qkv, 1, ns.quarter_q_v)
        whole_o = copies.local(ns.w_out.at[0], ns.wo_v.at[upper])
        whole_d = copies.local(ns.w_down.at[0], ns.wd_v.at[upper])
        quarter_u = quarter_of(ns, place, ns.w_up, 1, ns.quarter_u_v)
        line = [place.line(offset)[0] for offset in range(1, 8)]
        meet([*line, place.along_x, place.along_y])
        down_in = copies.remote(ns.w_down.at[0, y, x], ns.wd_v.at[upper, y, x], place.far)
        part_u.wait()
        up_spread = spread(copies, place, by_columns(ns.wu_v))
        down_spread = spread(copies, place, by_rows(ns.wd_v, place))
        next(up_spread)
        quarter_q.wait()
        arrange(ns.quarter_q_v, ns.deal_q_v, 6)
        q_deal = deal(copies, place, ns.deal_q_v, ns.wq_v.at[upper, t, y, x])
        next(q_deal)
        next(q_deal)
        q_spread = spread(copies, place, by_columns(ns.wq_v))
        u_deal = deal(copies, place, ns.deal_u_v, ns.next_u.at[upper, t])
        o_spread = spread(copies, place, by_rows(ns.next_o, place))
        rest = []

        def out_part():
            rest.append(copies.remote(ns.w_out.at[1, y, x], ns.next_o.at[upper, y, x], place.far))

        def deal_up():
            quarter_u.wait()
            arrange(ns.quarter_u_v, ns.deal_u_v, 2)
            next(u_deal)
            next(u_deal)

        def down_arrived():
            down_in.wait_recv()
            next(down_spread)

        def out_arrived():
            rest[0].wait_recv()
            next(o_spread)

        plan = Plan(
            [],
            [],
            [stages(up_spread)],
            [deal_up],
            [down_arrived],
            [stages(down_spread), out_part],
            [stages(q_deal), stages(q_spread)],
            [stages(q_spread)],
            [out_arrived],
            [],
            [stages(o_spread)],
            [stages(o_spread)],
        )
        ns.load.qkv_in.wait()
        ns.load.gains.wait()
        gain = rows_of(ns, 0)

        def wait_out():
            half_o.wait()
            whole_o.wait()
            copies.store(ns.wo_v, ns.wo)

        def wait_down():
            next(down_spread)
            whole_d.wait()
            copies.store(ns.wu_v, ns.wu)
            copies.store(ns.wd_v, ns.wd)

        def wait_next():
            next(q_spread)
            copies.store(ns.wq_v, ns.wq)

        down = fwd_mid(ns, place, gain, plan.tick, wait_out, lambda: next(up_spread), wait_down)
        copies.store(ns.mixed_v, ns.mixed)
        copies.store(ns.lse_v, ns.lse)
        copies.store(ns.attn_out_v, ns.attn_out)
        copies.store(ns.resid_v, ns.resid)
        copies.store(ns.mlp_v, ns.mlp)
        copies.store(ns.active_v, ns.active)
        copies.store(ns.slope_v, ns.slope)

        def block(stream):
            value = down.result(stream)
            ns.down_out_v[stream] = value
            hidden_out = ns.resid_v[stream] + norm(value, gain(3))
            ns.hidden_out_v[stream] = hidden_out
            return norm(hidden_out, gain(0, 1)).astype(BF)

        blocks = [functools.partial(block, stream) for stream in range(2)]
        next_qkv(ns, place, blocks, plan.tick, wait_next)
        copies.store(ns.down_out_v, ns.down_out)
        copies.store(ns.hidden_out_v, ns.hidden_out)
        plan.drain()
        next(u_deal)

    flops = 2 * length * width * (mixed_width + 2 * units + part)
    kernel, options = kernel_of(forward, inputs, outputs, scratch, 1, 80, 64, 62, flops)
    results = pl.pallas_call(kernel, **options)(*inputs.values())
    return named(outputs, results)


def turn_kernel(lower, gains, w_down, w_out, cotangent):
    hidden = lower.hidden_out
    width = hidden.shape[2]
    length, part = lower.qkv.shape
    mixed_width = part // 3
    inputs = dict(
        qkv_in=lower.qkv, gains=gains, hidden=hidden, cot=cotangent,
        part_u=lower.next_u, part_o=lower.next_o, w_down=w_down, w_out=w_out,
    )
    rows, units = lower.next_u.shape[2:]
    blocks = struct((2, TOK, width), F32)
    outputs = dict(
        out=struct((2, TOK, width), BF),
        lse=struct((length, 128), F32),
        mixed_grad=struct((length, mixed_width), BF),
        gd=by_device((units, width), 1),
        gu=by_device((width, units), 4),
        go=by_device((mixed_width, width), 1),
        dg=struct((8, width), F32),
    )
    kept = dict(
        qkv_in=lower.qkv,
        hidden=hidden,
        gains=gains,
        cot=cotangent,
        wd=struct((2, *w_down.shape[1:]), BF),
        wo=lower.next_o,
        wu=struct((2, 4, 2, 2, rows, units), BF),
        mixed=struct((length, mixed_width), BF),
        attn_out=blocks,
        resid=blocks,
        grad=blocks,
        mlp=struct((length, width), BF),
        active=struct((length, units), BF),
        slope=struct((length, units), BF),
        up_grad=struct((length, units), BF),
        down_out=blocks,
        down_grad=struct((length, width), BF),
        attn_grad=struct((length, width), BF),
    )
    scratch = held(outputs, kept)
    outputs |= dict(resid_grad=blocks)
    for name in (ATTN, DOWN, UP):
        scratch |= scatter_scratch(name, width)
    scratch |= reduce_scratch(D1, 1, units // 8, width, 1) | reduce_scratch(U1, 4, rows, units, 1)

    def turn(ns):
        place, copies = Place(), ns.copies
        upper, y, x = place.upper, place.y, place.x
        part_u = copies.local(ns.part_u, ns.wu_v.at[:, :, y, x])
        part_o = copies.local(ns.part_o.at[1 - upper], ns.wo_v.at[1 - upper])
        whole_o = copies.local(ns.w_out.at[1], ns.wo_v.at[upper])
        whole_d = copies.local(ns.w_down.at[1], ns.wd_v.at[upper])
        meet([place.core, place.near, place.far, place.along_x, place.along_y])
        down_in = copies.remote(ns.w_down.at[1, y, x], ns.wd_v.at[upper, y, x], place.far)
        part_u.wait()
        up_spread = spread(copies, place, by_columns(ns.wu_v))
        down_spread = spread(copies, place, by_rows(ns.wd_v, place))
        next(up_spread)
        ns.load.qkv_in.wait()
        far_in = []

        def bring():
            ns.load.cot.wait()
            far_in.append(copies.remote(ns.cot.at[1 - upper], ns.cot_far_v, place.far))

        def down_arrived():
            down_in.wait_recv()
            next(down_spread)

        plan = Plan(
            [],
            [],
            [stages(up_spread)],
            [],
            [down_arrived],
            [stages(down_spread), bring],
        )
        ns.load.gains.wait()
        ns.dg_v[...] = jnp.zeros_like(ns.dg_v)
        gain = rows_of(ns, 1)

        def wait_out():
            part_o.wait()
            whole_o.wait()

        def wait_down():
            next(down_spread)
            whole_d.wait()

        down = fwd_mid(
            ns, place, gain, plan.tick, wait_out, lambda: next(up_spread), wait_down
        )
        copies.store(ns.lse_v, ns.lse)
        far_in[0].wait_recv()

        def grad(stream):
            value = down.result(stream)
            ns.down_out_v[stream] = value
            own = jnp.where(upper == stream, ns.cot_v[stream], ns.cot_far_v[...])
            return own.astype(F32)

        def finish():
            for stream in range(2):
                out = ns.resid_v[stream] + norm(ns.down_out_v[stream], gain(3))
                ns.out_v[stream] = out.astype(BF)
            copies.store(ns.out_v.at[upper], ns.out.at[upper])
            far_in.append(copies.remote(ns.out_v.at[1 - upper], ns.out.at[upper], place.far))

        d_first, unused = reduce_rep(copies, place, ns.gd_v, ns, D1)
        u_first, unused = reduce_rep(copies, place, ns.gu_v, ns, U1)
        plan = Plan(
            [],
            [finish],
            [],
            [],
            [],
        )
        grads = [functools.partial(grad, stream) for stream in range(2)]
        bwd_mid(ns, place, 1, grads, plan.tick, stages(d_first), stages(u_first))
        copies.store(ns.go_v, ns.go)
        copies.store(ns.dg_v, ns.dg)
        next(d_first)
        copies.store(ns.gd_v, ns.gd)
        next(u_first)
        copies.store(ns.gu_v, ns.gu)
        far_in[1].wait_recv()

    scratch["cot_far_v"] = pltpu.VMEM((TOK, width), BF)
    flops = 6 * length * width * (mixed_width + 2 * units)
    kernel, options = kernel_of(turn, inputs, outputs, scratch, 2, 64, 64, 63, flops)
    results = pl.pallas_call(kernel, **options)(*inputs.values())
    return named(outputs, results)


def backward_kernel(begun, lower, turned):
    wo, wu, wd, wq = (matrix(value) for value in (lower.wo, lower.wu, lower.wd, lower.wq))
    width, units = wu.shape
    length, part = lower.qkv.shape
    mixed_width = wo.shape[0]
    inputs = dict(
        d1=turned.gd, u1=turned.gu, o1=turned.go, qkv_in=lower.qkv, lse=turned.lse,
        mixed_grad=turned.mixed_grad, dg=turned.dg, gains=begun.gains, wq=wq, normed=lower.normed,
        hidden=lower.hidden_out, grad=turned.resid_grad, down_out=lower.down_out, wd=wd,
        slope=lower.slope, wu=wu, active=lower.active, mlp=lower.mlp, resid=lower.resid,
        attn_out=lower.attn_out, wo=wo, mixed=lower.mixed,
    )
    blocks = struct((2, TOK, width), F32)
    kept = dict(
        gq=by_device(wq.shape, 4),
        gd=by_device(wd.shape, 1),
        gu=by_device(wu.shape, 4),
        go=by_device(wo.shape, 1),
        qkv_grad=struct(lower.qkv.shape, BF),
        dk=struct((length, mixed_width), F32),
        dv=struct((length, mixed_width), F32),
        down_grad=struct((length, width), BF),
        attn_grad=struct((length, width), BF),
    )
    outputs = dict(
        resid_grad=blocks,
        mixed_out=struct((length, mixed_width), BF),
        gd=kept["gd"],
        gu=kept["gu"],
        go=kept["go"],
        dg_out=turned.dg,
        full_d=struct((2, 2, 2, units // 16, width), BF),
        full_u=struct((2, 2, width // 32, 4 * units), BF),
        full_q=struct((2, 2, width // 32, 4 * part), BF),
        full_o=struct((2, 2, 2, mixed_width // 16, width), BF),
    )
    loaded = dict(inputs)
    del loaded["d1"], loaded["u1"]
    scratch = held(loaded, kept)
    for name in (QKV, UP):
        scratch |= scatter_scratch(name, width)
    rows = width // 32
    for name, count, high, wide, steps in (
        (D1, 1, units // 8, width, 2),
        (U1, 4, rows, units, 2),
        (Q1, 4, rows, part, 3),
        (O1, 1, mixed_width // 8, width, 3),
    ):
        scratch |= finish_scratch(name, count, high, wide)
        scratch |= reduce_scratch(name, count, high, wide, steps)
    scratch |= reduce_scratch(D0, 1, units // 8, width, 1)

    def backward(ns):
        place, copies = Place(), ns.copies
        ns.up_grad_v = ns.normed_v
        line = [place.line(offset)[0] for offset in range(1, 8)]
        meet([*line, place.along_x, place.along_y])
        unused, d1_second = reduce_rep(copies, place, ns.d1, ns, D1)
        unused, u1_second = reduce_rep(copies, place, ns.u1, ns, U1)
        o1_first, o1_second = reduce_rep(copies, place, ns.o1_v, ns, O1)
        q1_first, q1_second = reduce_rep(copies, place, ns.gq_v, ns, Q1)
        d0_first, unused = reduce_rep(copies, place, ns.gd_v, ns, D0)
        d1_line = line_rows(copies, place, ns, D1)
        u1_line = line_columns(copies, place, ns, U1)
        o1_line = line_rows(copies, place, ns, O1)
        q1_line = line_columns(copies, place, ns, Q1)
        d1_whole = whole_rows(copies, place, ns, D1, ns.full_d)
        u1_whole = whole_columns(copies, place, ns, U1, ns.full_u, 2)
        q1_whole = whole_columns(copies, place, ns, Q1, ns.full_q, 6)
        o1_whole = whole_rows(copies, place, ns, O1, ns.full_o)
        next(u1_second)
        next(d1_second)
        ns.load.o1.wait()
        next(o1_first)
        ns.load.qkv_in.wait()
        ns.load.lse.wait()
        ns.load.mixed_grad.wait()
        ns.load.dg.wait()
        plan = Plan(
            [stages(u1_second), stages(u1_line)],
            [],
            [stages(d1_second)],
            [stages(o1_first), stages(o1_second)],
            [],
            [],
            [stages(d1_line), stages(o1_second), stages(o1_line), stages(u1_line)]
            + [stages(u1_whole)],
            [stages(q1_first), stages(q1_second), stages(u1_whole)],
            [stages(q1_second), stages(q1_line), stages(d1_line), stages(d1_whole)],
            [stages(u1_whole), stages(d1_whole)],
            [],
            [stages(q1_line), stages(q1_whole), stages(o1_line), stages(o1_whole)],
            [stages(d1_whole)],
            [],
            [stages(d0_first), stages(q1_whole), stages(o1_whole)],
        )
        ns.load.gains.wait()
        grads = bwd_head(ns, place, 1, plan.tick, stages(q1_first), False)
        for copy in (ns.load.down_out, ns.load.wd, ns.load.slope, ns.load.wu, ns.load.active):
            copy.wait()
        for copy in (ns.load.mlp, ns.load.resid, ns.load.attn_out, ns.load.wo, ns.load.mixed):
            copy.wait()
        ns.mixed_grad = ns.mixed_out
        store_up = functools.partial(copies.store, ns.gu_v, ns.gu)
        bwd_mid(ns, place, 0, grads, plan.tick, stages(d0_first), store_up, (1, 0))
        plan.drain()
        copies.store(ns.go_v, ns.go)
        copies.store(ns.gd_v, ns.gd)
        copies.store(ns.dg_v, ns.dg_out)
        next(q1_whole)
        next(o1_whole)

    flops = 6 * length * width * (mixed_width + 2 * units) + 4 * length * width * part
    kernel, options = kernel_of(backward, inputs, outputs, scratch, 3, 128, 128, 63, flops)
    results = pl.pallas_call(kernel, **options)(*inputs.values())
    return named(outputs, results)


def last_kernel(begun, lower, back):
    wq = matrix(begun.wq)
    width, part = wq.shape
    length, mixed_width = back.mixed_out.shape
    units, rows = back.gu.shape[-1], width // 32
    inputs = dict(
        u0=back.gu, d0=back.gd, o0=back.go, qkv_in=begun.qkv, lse=lower.lse,
        mixed_grad=back.mixed_out, dg=back.dg_out, gains=begun.gains, normed=begun.normed, wq=wq,
        hidden=begun.hidden, grad=back.resid_grad,
    )
    outputs = dict(
        out=struct((2, TOK, width), BF),
        gain_grad=struct((8, TOK), F32),
        full_d=struct(back.full_d.shape, BF),
        full_u=struct(back.full_u.shape, BF),
        full_q=struct(back.full_q.shape, BF),
        full_o=struct(back.full_o.shape, BF),
    )
    kept = dict(
        out=outputs["out"],
        gq=by_device(wq.shape, 4),
        qkv_grad=struct(begun.qkv.shape, BF),
        dk=struct((length, mixed_width), F32),
        dv=struct((length, mixed_width), F32),
        dg_line=struct((8, 8, TOK), F32),
        dg_pass=struct((5, 8, TOK), F32),
    )
    loaded = dict(inputs)
    del loaded["d0"]
    scratch = held(loaded, kept)
    scratch |= scatter_scratch(QKV, width)
    for name, count, high, wide, steps in (
        (D0, 1, units // 8, width, 2),
        (U0, 4, rows, units, 3),
        (Q0, 4, rows, part, 3),
        (O0, 1, mixed_width // 8, width, 3),
    ):
        scratch |= reduce_scratch(name, count, high, wide, steps)
        scratch |= finish_scratch(name, count, high, wide)

    def last(ns):
        place, copies = Place(), ns.copies
        line = [place.line(offset)[0] for offset in range(1, 8)]
        meet([*line, place.along_x, place.along_y])
        unused, d0_second = reduce_rep(copies, place, ns.d0, ns, D0)
        u0_first, u0_second = reduce_rep(copies, place, ns.u0_v, ns, U0)
        o0_first, o0_second = reduce_rep(copies, place, ns.o0_v, ns, O0)
        q0_first, q0_second = reduce_rep(copies, place, ns.gq_v, ns, Q0)
        d0_line = line_rows(copies, place, ns, D0)
        o0_line = line_rows(copies, place, ns, O0)
        u0_line = line_columns(copies, place, ns, U0)
        q0_line = line_columns(copies, place, ns, Q0)
        d0_whole = whole_rows(copies, place, ns, D0, ns.full_d)
        o0_whole = whole_rows(copies, place, ns, O0, ns.full_o)
        u0_whole = whole_columns(copies, place, ns, U0, ns.full_u, 2)
        q0_whole = whole_columns(copies, place, ns, Q0, ns.full_q, 6)
        next(d0_second)
        ns.load.u0.wait()
        next(u0_first)
        ns.load.qkv_in.wait()
        ns.load.lse.wait()
        ns.load.mixed_grad.wait()
        ns.load.dg.wait()
        ns.load.o0.wait()
        plan = Plan(
            [stages(d0_second), stages(d0_line)],
            [],
            [],
            [],
            [],
            [stages(d0_line), stages(d0_whole), stages(u0_first), stages(u0_second)],
        )
        ns.load.gains.wait()
        grads = bwd_head(ns, place, 0, plan.tick, stages(q0_first), True)
        upper = place.upper
        ns.out_v[1] = grads[1]().astype(BF)
        for task in (q0_first, q0_second, o0_first):
            next(task)
        ns.out_v[0] = grads[0]().astype(BF)
        copies.store(ns.out_v.at[upper], ns.out.at[upper])
        gain_grad = gain_sum(ns, copies, place)
        next(gain_grad)
        moved = copies.remote(ns.out_v.at[1 - upper], ns.out.at[upper], place.far)
        for task in (
            d0_whole, u0_second, u0_line, q0_second, q0_line, o0_first, o0_second, gain_grad,
            u0_line, u0_whole, o0_second, o0_line, d0_whole, u0_whole, q0_line, q0_whole,
            o0_line, o0_whole, gain_grad, q0_whole, o0_whole, gain_grad, u0_whole, q0_whole,
            o0_whole,
        ):
            next(task)
        moved.wait_recv()

    flops = 4 * length * width * part
    kernel, options = kernel_of(last, inputs, outputs, scratch, 4, 128, 128, 60, flops)
    results = pl.pallas_call(kernel, **options)(*inputs.values())
    return named(outputs, results)


def gain_sum(ns, copies, place):
    def columns(grp):
        return pl.ds(pl.multiple_of(grp * TOK, TOK), TOK)

    moved = []
    for offset in range(1, 8):
        device, upper, t = place.line(offset)
        source = ns.dg_v.at[:, columns(upper * 4 + t)]
        moved.append(copies.remote(source, ns.dg_line_v.at[place.grp], device))
    ns.dg_line_v[place.grp] = ns.dg_v[:, columns(place.grp)]
    yield
    for copy in moved:
        copy.wait_recv()
    ns.dg_pass_v[0] = jnp.sum(ns.dg_line_v[...], axis=0)
    moved = copies.remote(ns.dg_pass_v.at[0], ns.dg_pass_v.at[1], place.along_x)
    yield
    moved.wait_recv()
    ns.dg_pass_v[2] = ns.dg_pass_v[0] + ns.dg_pass_v[1]
    moved = copies.remote(ns.dg_pass_v.at[2], ns.dg_pass_v.at[3], place.along_y)
    yield
    moved.wait_recv()
    ns.dg_pass_v[4] = ns.dg_pass_v[2] + ns.dg_pass_v[3]
    copies.store(ns.dg_pass_v.at[4], ns.gain_grad)
    yield


def body_pairs(block_in, cotangent, w_qkv, w_out, w_up, w_down, norm_gains):
    layers, rows, width = w_out.shape
    hidden_unit = w_down.shape[1]
    gain_part = jnp.transpose(norm_gains.astype(F32), (0, 2, 1)).reshape(layers * 4, rows)
    down_parts = w_down.reshape(layers, 2, 2, 2, hidden_unit // 8, width)
    out_parts = w_out.reshape(layers, 2, 2, 2, rows // 8, width)

    begun = start_kernel(block_in[:, 0], gain_part, w_qkv, w_up, out_parts)
    lower = forward_kernel(begun, w_qkv, w_up, down_parts, out_parts)
    turned = turn_kernel(lower, begun.gains, down_parts, out_parts, cotangent[:, 0])
    back = backward_kernel(begun, lower, turned)
    last = last_kernel(begun, lower, back)

    def whole(zero, one, like):
        return jnp.stack([zero, one]).reshape(like.shape).astype(F32)

    return (
        turned.out[:, None],
        last.out.astype(F32)[:, None],
        whole(last.full_q, back.full_q, w_qkv),
        whole(last.full_o, back.full_o, w_out),
        whole(last.full_u, back.full_u, w_up),
        whole(last.full_d, back.full_d, w_down),
        jnp.transpose(last.gain_grad.reshape(layers, 4, rows), (0, 2, 1)),
    )


def norm_apply(values, gains):
    return values * lax.rsqrt(jnp.mean(values * values, axis=-1, keepdims=True) + EPS) * gains


def inner_rows(left, right):
    return lax.dot_general(
        left, right, (((0,), (0,)), ((), ())), preferred_element_type=jnp.float32
    )


def times_trans(left, right):
    return lax.dot_general(
        left, right, (((1,), (1,)), ((), ())), preferred_element_type=jnp.float32
    )


def split_blocks(whole):
    length = whole.shape[0]
    width = min(512, length)
    count = length // width
    return (whole.reshape(count, width, HEADS, HDIM), width, count)


def block_at(blocks, index):
    return lax.dynamic_index_in_dim(blocks, index, 0, keepdims=False)


def key_scores(query, key_block, key_start, query_pos):
    scale = HDIM ** (-0.5)
    scores = (
        jnp.einsum("qhd,khd->hqk", query, key_block, preferred_element_type=jnp.float32) * scale
    )
    key_pos = key_start + jnp.arange(key_block.shape[0], dtype=jnp.int32)
    allowed = key_pos[None, :] <= query_pos[:, None]
    return (scores, allowed[None])


def attend_split(query, keys_all, values_all, query_pos):
    key_blocks, width, count = split_blocks(keys_all)
    value_blocks = split_blocks(values_all)[0]
    row_count = query.shape[0]
    upper = query_pos[row_count - 1] // width + 1

    def total_step(index, carry):
        running, total = carry
        scores, allowed = key_scores(query, block_at(key_blocks, index), index * width, query_pos)
        newest = jnp.maximum(running, jnp.max(jnp.where(allowed, scores, NEGATIVE), axis=-1))
        terms = jnp.where(allowed, jnp.exp(scores - newest[..., None]), 0.0)
        total = total * jnp.exp(running - newest) + jnp.sum(terms, axis=-1)
        return (newest, total)

    start_run = jnp.full((HEADS, row_count), NEGATIVE, jnp.float32)
    start_total = jnp.zeros((HEADS, row_count), jnp.float32)
    running, total = lax.fori_loop(0, upper, total_step, (start_run, start_total))
    log_total = running + jnp.log(total)

    def mix_step(index, accum):
        scores, allowed = key_scores(query, block_at(key_blocks, index), index * width, query_pos)
        probs = jnp.where(allowed, jnp.exp(scores - log_total[..., None]), 0.0)
        return accum + jnp.einsum(
            "hqk,khd->qhd",
            probs.astype(jnp.bfloat16),
            block_at(value_blocks, index),
            preferred_element_type=jnp.float32,
        )

    start_mix = jnp.zeros((row_count, HEADS, HDIM), jnp.float32)
    mixed = lax.fori_loop(0, upper, mix_step, start_mix)
    return (mixed.reshape(row_count, HEADS * HDIM), log_total)


def attend_back_split(query, keys_all, values_all, log_total, out_grad, delta, query_pos):
    key_blocks, width, count = split_blocks(keys_all)
    value_blocks = split_blocks(values_all)[0]
    row_count = query.shape[0]
    upper = query_pos[row_count - 1] // width + 1
    scale = HDIM ** (-0.5)

    def back_step(index, carry):
        query_acc, pieces = carry
        key_block = block_at(key_blocks, index)
        value_block = block_at(value_blocks, index)
        scores, allowed = key_scores(query, key_block, index * width, query_pos)
        probs = jnp.where(allowed, jnp.exp(scores - log_total[..., None]), 0.0)
        prob_grad = jnp.einsum(
            "qhd,khd->hqk", out_grad, value_block, preferred_element_type=jnp.float32
        )
        score_grad = (probs * (prob_grad - delta[..., None])).astype(jnp.bfloat16)
        query_acc = (
            query_acc
            + jnp.einsum("hqk,khd->qhd", score_grad, key_block, preferred_element_type=jnp.float32)
            * scale
        )
        key_grad = (
            jnp.einsum("hqk,qhd->khd", score_grad, query, preferred_element_type=jnp.float32)
            * scale
        )
        value_grad = jnp.einsum(
            "hqk,qhd->khd", probs.astype(jnp.bfloat16), out_grad, preferred_element_type=jnp.float32
        )
        joined = jnp.concatenate(
            [key_grad.reshape(width, HEADS * HDIM), value_grad.reshape(width, HEADS * HDIM)], axis=1
        )
        pieces = lax.dynamic_update_index_in_dim(pieces, joined, index, 0)
        return (query_acc, pieces)

    start_acc = jnp.zeros((row_count, HEADS, HDIM), jnp.float32)
    start_pieces = jnp.zeros((count, width, 2 * HEADS * HDIM), jnp.float32)
    query_grad, pieces = lax.fori_loop(0, upper, back_step, (start_acc, start_pieces))
    return (query_grad.reshape(row_count, HEADS * HDIM), pieces.reshape(-1, pieces.shape[-1]))


def layer_forward(hidden_in, weights, query_pos):
    w_qkv_full, w_out_full, w_up_full, w_down_full, gain_full = weights
    gains_f = gain_full.astype(jnp.float32)
    row_count = hidden_in.shape[0]
    width = w_out_full.shape[1]
    normed = norm_apply(hidden_in, gains_f[:, 0]).astype(jnp.bfloat16)
    qkv_low = jnp.dot(normed, w_qkv_full, preferred_element_type=jnp.float32).astype(jnp.bfloat16)
    query = qkv_low[:, :width]
    keys_all, values_all = (
        lax.all_gather(qkv_low[:, width : 2 * width], "grp", axis=0, tiled=True),
        lax.all_gather(qkv_low[:, 2 * width :], "grp", axis=0, tiled=True),
    )
    mixed, log_total = attend_split(
        query.reshape(row_count, HEADS, HDIM),
        keys_all.reshape(-1, HEADS, HDIM),
        values_all.reshape(-1, HEADS, HDIM),
        query_pos,
    )
    mixed_low = mixed.astype(jnp.bfloat16)
    attn_out = jnp.dot(mixed_low, w_out_full, preferred_element_type=jnp.float32)
    resid = hidden_in + norm_apply(attn_out, gains_f[:, 1])
    mlp_in = norm_apply(resid, gains_f[:, 2]).astype(jnp.bfloat16)
    up_out = jnp.dot(mlp_in, w_up_full, preferred_element_type=jnp.float32)
    active = jax.nn.gelu(up_out).astype(jnp.bfloat16)
    down_out = jnp.dot(active, w_down_full, preferred_element_type=jnp.float32)
    result = resid + norm_apply(down_out, gains_f[:, 3])
    kept = (
        hidden_in,
        normed,
        qkv_low,
        mixed,
        mixed_low,
        log_total,
        attn_out,
        resid,
        mlp_in,
        up_out,
        active,
        down_out,
    )
    return (result, kept)


def layer_backward(grad_out, weights, kept, query_pos):
    w_qkv_full, w_out_full, w_up_full, w_down_full, gain_full = weights
    (
        hidden_in,
        normed,
        qkv_low,
        mixed,
        mixed_low,
        log_total,
        attn_out,
        resid,
        mlp_in,
        up_out,
        active,
        down_out,
    ) = kept
    gains_f = gain_full.astype(jnp.float32)
    row_count = hidden_in.shape[0]
    width = w_out_full.shape[1]
    unused, puller = jax.vjp(norm_apply, down_out, gains_f[:, 3])
    down_grad, gain_four = puller(grad_out)
    down_low = down_grad.astype(jnp.bfloat16)
    w_down_grad = inner_rows(active, down_low)
    active_grad = times_trans(down_low, w_down_full)
    unused, puller = jax.vjp(jax.nn.gelu, up_out)
    up_low = puller(active_grad)[0].astype(jnp.bfloat16)
    w_up_grad = inner_rows(mlp_in, up_low)
    mlp_grad = times_trans(up_low, w_up_full)
    unused, puller = jax.vjp(norm_apply, resid, gains_f[:, 2])
    resid_part, gain_three = puller(mlp_grad)
    resid_grad = grad_out + resid_part
    unused, puller = jax.vjp(norm_apply, attn_out, gains_f[:, 1])
    attn_grad, gain_two = puller(resid_grad)
    attn_low = attn_grad.astype(jnp.bfloat16)
    w_out_grad = inner_rows(mixed_low, attn_low)
    mixed_grad = times_trans(attn_low, w_out_full).astype(jnp.bfloat16)
    keys_all, values_all = (
        lax.all_gather(qkv_low[:, width : 2 * width], "grp", axis=0, tiled=True),
        lax.all_gather(qkv_low[:, 2 * width :], "grp", axis=0, tiled=True),
    )
    delta = jnp.sum(
        (mixed_grad.astype(jnp.float32) * mixed).reshape(row_count, HEADS, HDIM), axis=-1
    ).T
    query_low = qkv_low[:, :width]
    query_grad, key_value_terms = attend_back_split(
        query_low.reshape(row_count, HEADS, HDIM),
        keys_all.reshape(-1, HEADS, HDIM),
        values_all.reshape(-1, HEADS, HDIM),
        log_total,
        mixed_grad.reshape(row_count, HEADS, HDIM),
        delta,
        query_pos,
    )
    key_value_grad = lax.psum_scatter(
        key_value_terms.astype(jnp.bfloat16), "grp", scatter_dimension=0, tiled=True
    ).astype(jnp.float32)
    qkv_grad = jnp.concatenate([query_grad, key_value_grad], axis=1).astype(jnp.bfloat16)
    w_qkv_grad = inner_rows(normed, qkv_grad)
    normed_grad = times_trans(qkv_grad, w_qkv_full)
    unused, puller = jax.vjp(norm_apply, hidden_in, gains_f[:, 0])
    input_part, gain_one = puller(normed_grad)
    gain_grad = jnp.stack([gain_one, gain_two, gain_three, gain_four], axis=1)
    return (resid_grad + input_part, (w_qkv_grad, w_out_grad, w_up_grad, w_down_grad, gain_grad))


def body_general(block_in, cotangent, w_qkv, w_out, w_up, w_down, norm_gains):
    layer_count = w_qkv.shape[0]
    micro_count = block_in.shape[0]
    row_count = block_in.shape[2]
    query_pos = lax.axis_index("grp") * row_count + jnp.arange(row_count, dtype=jnp.int32)
    totals = [None] * layer_count
    outputs = []
    input_grads = []
    for micro_idx in range(micro_count):
        hidden = block_in[micro_idx, 0].astype(jnp.float32)
        saved = []
        for layer_idx in range(layer_count):
            hidden, kept = layer_forward(
                hidden,
                (
                    lax.all_gather(w_qkv[layer_idx], "grp", axis=0, tiled=True),
                    lax.all_gather(w_out[layer_idx], "grp", axis=0, tiled=True),
                    lax.all_gather(w_up[layer_idx], "grp", axis=0, tiled=True),
                    lax.all_gather(w_down[layer_idx], "grp", axis=0, tiled=True),
                    lax.all_gather(norm_gains[layer_idx], "grp", axis=0, tiled=True),
                ),
                query_pos,
            )
            saved.append(kept)
        outputs.append(hidden.astype(jnp.bfloat16))
        grad_flow = cotangent[micro_idx, 0].astype(jnp.float32)
        for layer_idx in reversed(range(layer_count)):
            grad_flow, parts = layer_backward(
                grad_flow,
                (
                    lax.all_gather(w_qkv[layer_idx], "grp", axis=0, tiled=True),
                    lax.all_gather(w_out[layer_idx], "grp", axis=0, tiled=True),
                    lax.all_gather(w_up[layer_idx], "grp", axis=0, tiled=True),
                    lax.all_gather(w_down[layer_idx], "grp", axis=0, tiled=True),
                    lax.all_gather(norm_gains[layer_idx], "grp", axis=0, tiled=True),
                ),
                saved[layer_idx],
                query_pos,
            )
            if totals[layer_idx] is None:
                totals[layer_idx] = parts
            else:
                totals[layer_idx] = tuple(
                    (left + right for left, right in zip(totals[layer_idx], parts))
                )
        input_grads.append(grad_flow)
    reduced = []
    for layer_idx in range(layer_count):
        accum = totals[layer_idx]
        shards = (
            lax.psum_scatter(
                accum[0].astype(jnp.bfloat16), "grp", scatter_dimension=0, tiled=True
            ).astype(jnp.float32),
            lax.psum_scatter(
                accum[1].astype(jnp.bfloat16), "grp", scatter_dimension=0, tiled=True
            ).astype(jnp.float32),
            lax.psum_scatter(
                accum[2].astype(jnp.bfloat16), "grp", scatter_dimension=0, tiled=True
            ).astype(jnp.float32),
            lax.psum_scatter(
                accum[3].astype(jnp.bfloat16), "grp", scatter_dimension=0, tiled=True
            ).astype(jnp.float32),
            lax.psum_scatter(
                accum[4].astype(jnp.bfloat16), "grp", scatter_dimension=0, tiled=True
            ).astype(jnp.float32),
        )
        reduced.append(
            (
                lax.psum(shards[0].astype(jnp.bfloat16), "rep").astype(jnp.float32),
                lax.psum(shards[1].astype(jnp.bfloat16), "rep").astype(jnp.float32),
                lax.psum(shards[2].astype(jnp.bfloat16), "rep").astype(jnp.float32),
                lax.psum(shards[3].astype(jnp.bfloat16), "rep").astype(jnp.float32),
                lax.psum(shards[4].astype(jnp.bfloat16), "rep").astype(jnp.float32),
            )
        )
    block_out = jnp.stack(outputs)[:, None]
    block_in_grad = jnp.stack(input_grads)[:, None]
    stacked = [
        jnp.stack([reduced[layer_idx][member] for layer_idx in range(layer_count)])
        for member in range(5)
    ]
    return (block_out, block_in_grad, stacked[0], stacked[1], stacked[2], stacked[3], stacked[4])


def solution(mesh):
    rep_size, grp_size = mesh.shape["rep"], mesh.shape["grp"]

    def body(block_in, cotangent, w_qkv, w_out, w_up, w_down, norm_gains):
        sizes = (rep_size, grp_size, block_in.shape[0], w_qkv.shape[0], block_in.shape[2])
        fits = sizes == (4, 8, 2, 2, TOK)
        chosen = body_pairs if fits else body_general
        return chosen(block_in, cotangent, w_qkv, w_out, w_up, w_down, norm_gains)

    tokens = P(None, "rep", "grp", None)
    rows = P(None, "grp", None)
    return jax.shard_map(
        body,
        mesh=mesh,
        in_specs=(tokens, tokens, rows, rows, rows, rows, rows),
        out_specs=(tokens, tokens, rows, rows, rows, rows, rows),
        check_vma=False,
    )
```

profile of v0, /device:TPU:0, one launch (start us, length us, event | category | flops | bytes accessed | tf_op | source)
XLA Modules:
  0.0 436.9 jit_solution(16878243625768918877)
XLA Ops:
  0.6 1.3 reshape.76
  1.9 48.3 %start.1 = (bf16[2,128,1024]{2,1,0:T(8,128)(2,1)}, f32[8,1024]{1,0:T(8,128)}, bf16[1024,1024]{1,0:T(8,128)(2,1)}, bf16[1024,768]{1,0:T(8,128)(2,1)}, bf16[2,4,2,...) custom-call(bf16[2,128,1024]{2,1,0:T(8,128)(2,1)} %bitcast.46, ...), custom_call_target="tpu_custom_call" | custom-call | flops 1610612736 | bytes 11309056 | tf_op jit(solution)/shard_map/start/pallas_call | solution.py:886
  50.2 80.1 %forward.1 = (bf16[1024,256]{1,0:T(8,128)(2,1)}, f32[1024,128]{1,0:T(8,128)}, f32[2,128,1024]{2,1,0:T(8,128)}, f32[2,128,1024]{2,1,0:T(8,128)}, bf16[1024,1024]{...) custom-call(bf16[1024,768]{1,0:T(8,128)(2,1)} %get-tuple-element.55., ...), custom_call_target="tpu_custom_call" | custom-call | flops 6442450944 | bytes 31752192 | tf_op jit(solution)/shard_map/forward/pallas_call | solution.py:1033
  130.2 109.6 %turn.1 = (bf16[2,128,1024]{2,1,0:T(8,128)(2,1)}, f32[1024,128]{1,0:T(8,128)}, bf16[1024,256]{1,0:T(8,128)(2,1)}, bf16[2,1,2,2,128,1024]{5,4,3,2,1,0:T(8,128)(2,...) custom-call(bf16[1024,768]{1,0:T(8,128)(2,1)} %get-tuple-element.60., ...), custom_call_target="tpu_custom_call" | custom-call | flops 14495514624 | bytes 14221312 | tf_op jit(solution)/shard_map/turn/pallas_call | solution.py:1168
  239.8 95.3 %backward.1 = (f32[2,128,1024]{2,1,0:T(8,128)}, bf16[1024,256]{1,0:T(8,128)(2,1)}, bf16[2,1,2,2,128,1024]{5,4,3,2,1,0:T(8,128)(2,1)}, bf16[2,4,2,2,32,1024]{5,4,...) custom-call(bf16[2,1,2,2,128,1024]{5,4,3,2,1,0:T(8,128)(2,1)} %get-t, ...), custom_call_target="tpu_custom_call" | custom-call | flops 17716740096 | bytes 37322752 | tf_op jit(solution)/shard_map/backward/pallas_call | solution.py:1286
  335.1 0.0 copy-start.7
  335.1 88.5 %last.1 = (bf16[2,128,1024]{2,1,0:T(8,128)(2,1)}, f32[8,128]{1,0:T(8,128)}, bf16[2,2,2,64,1024]{4,3,2,1,0:T(8,128)(2,1)}, bf16[2,2,32,4096]{3,2,1,0:T(8,128)(2,1...) custom-call(bf16[2,4,2,2,32,1024]{5,4,3,2,1,0:T(8,128)(2,1)} %get-tuple-element.84.refs_0_, ...), custom_call_target="tpu_custom_call" | custom-call | flops 3221225472 | bytes 16322560 | tf_op jit(solution)/shard_map/last/pallas_call | solution.py:1384
  423.6 0.0 copy-start.4
  423.6 0.0 copy-start.5
  423.7 2.2 bitcast_convert_fusion
  425.9 0.0 copy-done.7
  425.9 2.0 maximum_convert_fusion.3
  427.9 0.0 copy-done.4
  427.9 0.0 copy-done.5
  427.9 0.0 copy-start.1
  427.9 0.0 copy-start.3
  427.9 1.9 maximum_convert_fusion.2
  429.8 0.0 copy-done.1
  429.8 0.7 copy-done.3
  430.4 0.0 copy-start
  430.4 0.0 copy-start.2
  430.4 2.3 maximum_convert_fusion
  432.7 0.0 copy-done
  432.7 0.1 copy-done.2
  432.8 0.0 copy-start.6
  432.8 0.0 copy-start.8
  432.8 2.3 maximum_convert_fusion.1
  435.1 0.0 copy-done.6
  435.1 0.8 copy.18
  435.9 0.0 copy-done.8
  435.9 0.6 copy.19
Async XLA Ops:
  335.1 90.8 %copy-start.7 = (bf16[2,2,2,16,1024]{4,3,2,1,0:T(8,128)(2,1)S(1)}, bf16[2,2,2,16,1024]{4,3,2,1,0:T(8,128)(2,1)}, u32[]{:S(2)}) copy-start(bf16[2,2,2,16,1024]{4,3,2,1,0:T(8,128)(2,1)} %get-tuple-element.97) | copy-start | bytes 786436
  423.6 4.3 copy-start.4
  423.6 4.2 copy-start.5
  427.9 1.9 copy-start.1
  427.9 2.5 copy-start.3
  430.4 2.3 copy-start
  430.4 2.4 copy-start.2
  432.8 2.3 copy-start.6
  432.8 3.1 copy-start.8
where the time goes:
time: 445 us; the launch traced here: 437 us
  Pallas kernels  422 us (95%)
  other arithmetic  11.9 us (3%)
    pallas_call x1, Pallas kernels, turn_kernel(): results = pl.pallas_call(kernel, **options)(*inputs.values())  110 us
    pallas_call x1, Pallas kernels, backward_kernel(): results = pl.pallas_call(kernel, **options)(*inputs.values())  95.3 us
    pallas_call x1, Pallas kernels, last_kernel(): results = pl.pallas_call(kernel, **options)(*inputs.values())  88.5 us
    pallas_call x1, Pallas kernels, forward_kernel(): results = pl.pallas_call(kernel, **options)(*inputs.values())  80.1 us
    pallas_call x1, Pallas kernels, start_kernel(): results = pl.pallas_call(kernel, **options)(*inputs.values())  48.3 us

commit v1 on v0

--- a/solution.py
+++ b/solution.py
@@ -157,7 +157,7 @@
 class Copies:
     def __init__(self, send, recv, here):
         self.sems, self.here = (send, recv), here
-        self.sent, self.local_count, self.stores = [], 0, []
+        self.sent, self.local_count, self.stores, self.done = [], 0, [], set()
 
     def remote(self, source, target, device):
         at = len(self.sent)
@@ -184,9 +184,16 @@
     def store(self, source, target):
         self.stores.append(self.local(source, target))
 
+    def both(self, *copies):
+        for copy in copies:
+            copy.wait_recv()
+            copy.wait_send()
+            self.done.add(id(copy))
+
     def finish(self):
         for copy in self.sent:
-            copy.wait_send()
+            if id(copy) not in self.done:
+                copy.wait_send()
         for copy in self.stores:
             copy.wait()
 
@@ -260,8 +267,7 @@
         first = copies.remote(grad.at[0, :, :, 1 - x], one.at[0], place.along_x)
         second = copies.remote(grad.at[1, :, 1 - y], one.at[1], place.along_y)
         yield
-        first.wait_recv()
-        second.wait_recv()
+        copies.both(first, second)
         for i in range(count):
             for j in range(2):
                 grad[0, i, j, x] = add_low(grad[0, i, j, x], one[0, i, j])
@@ -274,8 +280,7 @@
         second = copies.remote(grad.at[1, :, y, 1 - x], two.at[1], place.along_x)
         own = [copies.local(grad.at[half, :, y, x], total.at[half]) for half in range(2)]
         yield
-        first.wait_recv()
-        second.wait_recv()
+        copies.both(first, second)
         for half in range(2):
             own[half].wait()
             for i in range(count):
@@ -1078,7 +1083,7 @@
     outputs |= dict(resid_grad=blocks)
     for name in (ATTN, DOWN, UP):
         scratch |= scatter_scratch(name, width)
-    scratch |= reduce_scratch(D1, 1, units // 8, width, 1) | reduce_scratch(U1, 4, rows, units, 1)
+    scratch |= reduce_scratch(D1, 1, units // 8, width, 1)
 
     def turn(ns):
         place, copies = Place(), ns.copies
@@ -1140,11 +1145,9 @@
             for stream in range(2):
                 out = ns.resid_v[stream] + norm(ns.down_out_v[stream], gain(3))
                 ns.out_v[stream] = out.astype(BF)
-            copies.store(ns.out_v.at[upper], ns.out.at[upper])
-            far_in.append(copies.remote(ns.out_v.at[1 - upper], ns.out.at[upper], place.far))
+            copies.store(ns.out_v, ns.out)
 
         d_first, unused = reduce_rep(copies, place, ns.gd_v, ns, D1)
-        u_first, unused = reduce_rep(copies, place, ns.gu_v, ns, U1)
         plan = Plan(
             [],
             [finish],
@@ -1153,14 +1156,12 @@
             [],
         )
         grads = [functools.partial(grad, stream) for stream in range(2)]
-        bwd_mid(ns, place, 1, grads, plan.tick, stages(d_first), stages(u_first))
+        store_up = functools.partial(copies.store, ns.gu_v, ns.gu)
+        bwd_mid(ns, place, 1, grads, plan.tick, stages(d_first), store_up)
         copies.store(ns.go_v, ns.go)
         copies.store(ns.dg_v, ns.dg)
         next(d_first)
         copies.store(ns.gd_v, ns.gd)
-        next(u_first)
-        copies.store(ns.gu_v, ns.gu)
-        far_in[1].wait_recv()
 
     scratch["cot_far_v"] = pltpu.VMEM((TOK, width), BF)
     flops = 6 * length * width * (mixed_width + 2 * units)
@@ -1175,7 +1176,7 @@
     length, part = lower.qkv.shape
     mixed_width = wo.shape[0]
     inputs = dict(
-        d1=turned.gd, u1=turned.gu, o1=turned.go, qkv_in=lower.qkv, lse=turned.lse,
+        gu=turned.gu, d1=turned.gd, o1=turned.go, qkv_in=lower.qkv, lse=turned.lse,
         mixed_grad=turned.mixed_grad, dg=turned.dg, gains=begun.gains, wq=wq, normed=lower.normed,
         hidden=lower.hidden_out, grad=turned.resid_grad, down_out=lower.down_out, wd=wd,
         slope=lower.slope, wu=wu, active=lower.active, mlp=lower.mlp, resid=lower.resid,
@@ -1197,7 +1198,7 @@
         resid_grad=blocks,
         mixed_out=struct((length, mixed_width), BF),
         gd=kept["gd"],
-        gu=kept["gu"],
+        up_out=kept["gu"],
         go=kept["go"],
         dg_out=turned.dg,
         full_d=struct((2, 2, 2, units // 16, width), BF),
@@ -1206,14 +1207,14 @@
         full_o=struct((2, 2, 2, mixed_width // 16, width), BF),
     )
     loaded = dict(inputs)
-    del loaded["d1"], loaded["u1"]
+    del loaded["d1"]
     scratch = held(loaded, kept)
     for name in (QKV, UP):
         scratch |= scatter_scratch(name, width)
     rows = width // 32
     for name, count, high, wide, steps in (
         (D1, 1, units // 8, width, 2),
-        (U1, 4, rows, units, 2),
+        (U1, 4, rows, units, 3),
         (Q1, 4, rows, part, 3),
         (O1, 1, mixed_width // 8, width, 3),
     ):
@@ -1227,7 +1228,7 @@
         line = [place.line(offset)[0] for offset in range(1, 8)]
         meet([*line, place.along_x, place.along_y])
         unused, d1_second = reduce_rep(copies, place, ns.d1, ns, D1)
-        unused, u1_second = reduce_rep(copies, place, ns.u1, ns, U1)
+        u1_first, u1_second = reduce_rep(copies, place, ns.gu_v, ns, U1)
         o1_first, o1_second = reduce_rep(copies, place, ns.o1_v, ns, O1)
         q1_first, q1_second = reduce_rep(copies, place, ns.gq_v, ns, Q1)
         d0_first, unused = reduce_rep(copies, place, ns.gd_v, ns, D0)
@@ -1239,31 +1240,31 @@
         u1_whole = whole_columns(copies, place, ns, U1, ns.full_u, 2)
         q1_whole = whole_columns(copies, place, ns, Q1, ns.full_q, 6)
         o1_whole = whole_rows(copies, place, ns, O1, ns.full_o)
-        next(u1_second)
         next(d1_second)
+        ns.load.gu.wait()
+        next(u1_first)
         ns.load.o1.wait()
-        next(o1_first)
         ns.load.qkv_in.wait()
         ns.load.lse.wait()
         ns.load.mixed_grad.wait()
         ns.load.dg.wait()
         plan = Plan(
-            [stages(u1_second), stages(u1_line)],
-            [],
-            [stages(d1_second)],
-            [stages(o1_first), stages(o1_second)],
+            [stages(d1_second), stages(d1_line)],
             [],
             [],
-            [stages(d1_line), stages(o1_second), stages(o1_line), stages(u1_line)]
-            + [stages(u1_whole)],
-            [stages(q1_first), stages(q1_second), stages(u1_whole)],
-            [stages(q1_second), stages(q1_line), stages(d1_line), stages(d1_whole)],
-            [stages(u1_whole), stages(d1_whole)],
+            [stages(u1_first), stages(u1_second), stages(o1_first)],
             [],
-            [stages(q1_line), stages(q1_whole), stages(o1_line), stages(o1_whole)],
-            [stages(d1_whole)],
             [],
-            [stages(d0_first), stages(q1_whole), stages(o1_whole)],
+            [stages(u1_second), stages(u1_line), stages(d1_line), stages(d1_whole)],
+            [stages(o1_first), stages(o1_second), stages(q1_first), stages(q1_second)],
+            [stages(d1_whole), stages(u1_line), stages(u1_whole)]
+            + [stages(q1_second), stages(q1_line)],
+            [stages(o1_second), stages(o1_line)],
+            [stages(d1_whole), stages(u1_whole), stages(q1_line), stages(q1_whole)],
+            [],
+            [stages(o1_line), stages(o1_whole), stages(q1_whole)],
+            [stages(u1_whole)],
+            [stages(d0_first), stages(o1_whole)],
         )
         ns.load.gains.wait()
         grads = bwd_head(ns, place, 1, plan.tick, stages(q1_first), False)
@@ -1272,7 +1273,7 @@
         for copy in (ns.load.mlp, ns.load.resid, ns.load.attn_out, ns.load.wo, ns.load.mixed):
             copy.wait()
         ns.mixed_grad = ns.mixed_out
-        store_up = functools.partial(copies.store, ns.gu_v, ns.gu)
+        store_up = functools.partial(copies.store, ns.gu_v, ns.up_out)
         bwd_mid(ns, place, 0, grads, plan.tick, stages(d0_first), store_up, (1, 0))
         plan.drain()
         copies.store(ns.go_v, ns.go)
@@ -1287,18 +1288,19 @@
     return named(outputs, results)
 
 
-def last_kernel(begun, lower, back):
+def last_kernel(begun, lower, turned, back):
     wq = matrix(begun.wq)
     width, part = wq.shape
     length, mixed_width = back.mixed_out.shape
-    units, rows = back.gu.shape[-1], width // 32
+    units, rows = back.up_out.shape[-1], width // 32
     inputs = dict(
-        u0=back.gu, d0=back.gd, o0=back.go, qkv_in=begun.qkv, lse=lower.lse,
+        u0=back.up_out, d0=back.gd, o0=back.go, qkv_in=begun.qkv, lse=lower.lse,
         mixed_grad=back.mixed_out, dg=back.dg_out, gains=begun.gains, normed=begun.normed, wq=wq,
-        hidden=begun.hidden, grad=back.resid_grad,
+        hidden=begun.hidden, grad=back.resid_grad, second=turned.out,
     )
     outputs = dict(
         out=struct((2, TOK, width), BF),
+        block_out=struct((2, TOK, width), BF),
         gain_grad=struct((8, TOK), F32),
         full_d=struct(back.full_d.shape, BF),
         full_u=struct(back.full_u.shape, BF),
@@ -1343,6 +1345,8 @@
         o0_whole = whole_rows(copies, place, ns, O0, ns.full_o)
         u0_whole = whole_columns(copies, place, ns, U0, ns.full_u, 2)
         q0_whole = whole_columns(copies, place, ns, Q0, ns.full_q, 6)
+        upper = place.upper
+        second = copies.remote(ns.second.at[1 - upper], ns.block_out.at[upper], place.far)
         next(d0_second)
         ns.load.u0.wait()
         next(u0_first)
@@ -1355,29 +1359,33 @@
             [stages(d0_second), stages(d0_line)],
             [],
             [],
+            [stages(u0_first), stages(u0_second)],
+            [stages(d0_line), stages(d0_whole)],
             [],
-            [],
-            [stages(d0_line), stages(d0_whole), stages(u0_first), stages(u0_second)],
         )
         ns.load.gains.wait()
         grads = bwd_head(ns, place, 0, plan.tick, stages(q0_first), True)
-        upper = place.upper
+        ns.load.second.wait()
+        copies.store(ns.second_v.at[upper], ns.block_out.at[upper])
         ns.out_v[1] = grads[1]().astype(BF)
-        for task in (q0_first, q0_second, o0_first):
+        for task in (u0_second, u0_line, q0_first, q0_second, o0_first, d0_whole):
             next(task)
         ns.out_v[0] = grads[0]().astype(BF)
         copies.store(ns.out_v.at[upper], ns.out.at[upper])
         gain_grad = gain_sum(ns, copies, place)
-        next(gain_grad)
+        for task in (
+            gain_grad, q0_second, q0_line, o0_first, o0_second, u0_line, u0_whole, d0_whole,
+            gain_grad, o0_second, o0_line,
+        ):
+            next(task)
         moved = copies.remote(ns.out_v.at[1 - upper], ns.out.at[upper], place.far)
         for task in (
-            d0_whole, u0_second, u0_line, q0_second, q0_line, o0_first, o0_second, gain_grad,
-            u0_line, u0_whole, o0_second, o0_line, d0_whole, u0_whole, q0_line, q0_whole,
-            o0_line, o0_whole, gain_grad, q0_whole, o0_whole, gain_grad, u0_whole, q0_whole,
-            o0_whole,
+            u0_whole, q0_line, q0_whole, o0_line, o0_whole, gain_grad, u0_whole, q0_whole,
+            o0_whole, gain_grad, q0_whole, o0_whole,
         ):
             next(task)
         moved.wait_recv()
+        second.wait_recv()
 
     flops = 4 * length * width * part
     kernel, options = kernel_of(last, inputs, outputs, scratch, 4, 128, 128, 60, flops)
@@ -1422,13 +1430,13 @@
     lower = forward_kernel(begun, w_qkv, w_up, down_parts, out_parts)
     turned = turn_kernel(lower, begun.gains, down_parts, out_parts, cotangent[:, 0])
     back = backward_kernel(begun, lower, turned)
-    last = last_kernel(begun, lower, back)
+    last = last_kernel(begun, lower, turned, back)
 
     def whole(zero, one, like):
         return jnp.stack([zero, one]).reshape(like.shape).astype(F32)
 
     return (
-        turned.out[:, None],
+        last.block_out[:, None],
         last.out.astype(F32)[:, None],
         whole(last.full_q, back.full_q, w_qkv),
         whole(last.full_o, back.full_o, w_out),

time: 445 us -> 427 us (0.960)
  Pallas kernels: 422 us -> 404 us
    pallas_call x1, Pallas kernels: 110 us -> 98.7 us  [turn_kernel(): results = pl.pallas_call(kernel, **options)(*inputs.values())]
    pallas_call x1, Pallas kernels: 88.5 us -> 80.6 us  [last_kernel(): results = pl.pallas_call(kernel, **options)(*inputs.values())]
where the time goes in v1:
time: 427 us; the launch traced here: 419 us
  Pallas kernels  404 us (95%)
  other arithmetic  11.9 us (3%)
    pallas_call x1, Pallas kernels, turn_kernel(): results = pl.pallas_call(kernel, **options)(*inputs.values())  98.7 us
    pallas_call x1, Pallas kernels, backward_kernel(): results = pl.pallas_call(kernel, **options)(*inputs.values())  95.8 us
    pallas_call x1, Pallas kernels, last_kernel(): results = pl.pallas_call(kernel, **options)(*inputs.values())  80.6 us
    pallas_call x1, Pallas kernels, forward_kernel(): results = pl.pallas_call(kernel, **options)(*inputs.values())  80.1 us
    pallas_call x1, Pallas kernels, start_kernel(): results = pl.pallas_call(kernel, **options)(*inputs.values())  48.3 us
    convert_element_type x4, other arithmetic, whole(): return jnp.stack([zero, one]).reshape(like.shape).astype(F32)  8.54 us

profile of v1, /device:TPU:0, one launch (start us, length us, event | category | flops | bytes accessed | tf_op | source)
XLA Modules:
  0.0 418.8 jit_solution(12602245107339135659)
XLA Ops:
  0.6 1.3 reshape.76
  1.9 48.3 %start.1 = (bf16[2,128,1024]{2,1,0:T(8,128)(2,1)}, f32[8,1024]{1,0:T(8,128)}, bf16[1024,1024]{1,0:T(8,128)(2,1)}, bf16[1024,768]{1,0:T(8,128)(2,1)}, bf16[2,4,2,...) custom-call(bf16[2,128,1024]{2,1,0:T(8,128)(2,1)} %bitcast.46, ...), custom_call_target="tpu_custom_call" | custom-call | flops 1610612736 | bytes 11309056 | tf_op jit(solution)/shard_map/start/pallas_call | solution.py:891
  50.2 80.1 %forward.1 = (bf16[1024,256]{1,0:T(8,128)(2,1)}, f32[1024,128]{1,0:T(8,128)}, f32[2,128,1024]{2,1,0:T(8,128)}, f32[2,128,1024]{2,1,0:T(8,128)}, bf16[1024,1024]{...) custom-call(bf16[1024,768]{1,0:T(8,128)(2,1)} %get-tuple-element.56., ...), custom_call_target="tpu_custom_call" | custom-call | flops 6442450944 | bytes 31752192 | tf_op jit(solution)/shard_map/forward/pallas_call | solution.py:1038
  130.2 98.7 %turn.1 = (bf16[2,128,1024]{2,1,0:T(8,128)(2,1)}, f32[1024,128]{1,0:T(8,128)}, bf16[1024,256]{1,0:T(8,128)(2,1)}, bf16[2,1,2,2,128,1024]{5,4,3,2,1,0:T(8,128)(2,...) custom-call(bf16[1024,768]{1,0:T(8,128)(2,1)} %get-tuple-element.61., ...), custom_call_target="tpu_custom_call" | custom-call | flops 14495514624 | bytes 14221312 | tf_op jit(solution)/shard_map/turn/pallas_call | solution.py:1169
  229.0 95.8 %backward.1 = (f32[2,128,1024]{2,1,0:T(8,128)}, bf16[1024,256]{1,0:T(8,128)(2,1)}, bf16[2,1,2,2,128,1024]{5,4,3,2,1,0:T(8,128)(2,1)}, bf16[2,4,2,2,32,1024]{5,4,...) custom-call(bf16[2,4,2,2,32,1024]{5,4,3,2,1,0:T(8,128)(2,1)} %get-tu, ...), custom_call_target="tpu_custom_call" | custom-call | flops 17716740096 | bytes 37322752 | tf_op jit(solution)/shard_map/backward/pallas_call | solution.py:1287
  324.8 0.0 copy-start.7
  324.8 80.6 %last.1 = (bf16[2,128,1024]{2,1,0:T(8,128)(2,1)}, bf16[2,128,1024]{2,1,0:T(8,128)(2,1)}, f32[8,128]{1,0:T(8,128)}, bf16[2,2,2,64,1024]{4,3,2,1,0:T(8,128)(2,1)},...) custom-call(bf16[2,4,2,2,32,1024]{5,4,3,2,1,0:T(8,128)(2,1)} %get-tuple-ele, ...), custom_call_target="tpu_custom_call" | custom-call | flops 3221225472 | bytes 17371136 | tf_op jit(solution)/shard_map/last/pallas_call | solution.py:1392
  405.5 0.0 copy-start.4
  405.5 0.0 copy-start.5
  405.5 0.0 copy-done.7
  405.5 2.1 maximum_convert_fusion.3
  407.6 2.1 bitcast_convert_fusion
  409.7 0.0 copy-done.4
  409.7 0.0 copy-done.5
  409.7 0.0 copy-start.1
  409.7 0.0 copy-start.3
  409.7 1.9 maximum_convert_fusion.2
  411.6 0.0 copy-done.1
  411.6 0.7 copy-done.3
  412.3 0.0 copy-start
  412.3 0.0 copy-start.2
  412.3 2.3 maximum_convert_fusion
  414.6 0.0 copy-done
  414.6 0.1 copy-done.2
  414.7 0.0 copy-start.6
  414.7 0.0 copy-start.8
  414.7 2.3 maximum_convert_fusion.1
  417.0 0.0 copy-done.6
  417.0 0.8 copy.18
  417.8 0.0 copy-done.8
  417.8 0.6 copy.19
Async XLA Ops:
  324.8 80.7 %copy-start.7 = (bf16[2,2,2,16,1024]{4,3,2,1,0:T(8,128)(2,1)S(1)}, bf16[2,2,2,16,1024]{4,3,2,1,0:T(8,128)(2,1)}, u32[]{:S(2)}) copy-start(bf16[2,2,2,16,1024]{4,3,2,1,0:T(8,128)(2,1)} %get-tuple-element.99) | copy-start | bytes 786436
  405.5 4.3 %copy-start.4 = (bf16[2,2,32,3072]{3,2,1,0:T(8,128)(2,1)S(1)}, bf16[2,2,32,3072]{3,2,1,0:T(8,128)(2,1)}, u32[]{:S(2)}) copy-start(bf16[2,2,32,3072]{3,2,1,0:T(8,128)(2,1)} %get-tuple-element.97) | copy-start | bytes 2359300
  405.5 4.3 %copy-start.5 = (bf16[2,2,32,3072]{3,2,1,0:T(8,128)(2,1)S(1)}, bf16[2,2,32,3072]{3,2,1,0:T(8,128)(2,1)}, u32[]{:S(2)}) copy-start(bf16[2,2,32,3072]{3,2,1,0:T(8,128)(2,1)} %get-tuple-element.96) | copy-start | bytes 2359300
  409.7 1.9 copy-start.1
  409.7 2.5 copy-start.3
  412.3 2.3 copy-start
  412.3 2.4 copy-start.2
  414.7 2.3 copy-start.6
  414.7 3.1 copy-start.8
